TPU v7x, 256 devices: a whole 4x4x8 slice. The times are simulated.
256 devices in a mesh: clique: 8 (over y_hi, x), copy: 32 (over z, y_lo, core).
Axes of the slice: x: 4, y: 4 (y_hi: 2, y_lo: 2; y = y_hi * 2 + y_lo), z: 8, core: 2. Of those that a mesh axis runs over, the one named last changes fastest.
Arguments:
- out_grad: bfloat16 [524288, 512], P(('clique', 'copy')), may hold values from -6 to 6
- pre_act: bfloat16 [524288, 512], P(('clique', 'copy')), may hold values from -6 to 6
- batch_count: int32 [256], P(('clique', 'copy')), may hold values from 1024 to 2048, as said below
- layer_two: bfloat16 [512, 512], replicated, may hold values from -0.25 to 0.25
- hot_slots: int32 [524288, 10], P(('clique', 'copy')), may hold values from 0 to 4095
- cold_index: int32 [524288, 15], P(('clique', 'copy')), may hold values from 0 to 2047
- hot_feats: bfloat16 [4096, 768], P('clique'), may hold values from -6 to 6
- cold_feats: bfloat16 [524288, 768], P(('clique', 'copy')), may hold values from -6 to 6
Outputs:
- grad_one: float32 [768, 512], replicated
- grad_two: float32 [512, 512], replicated
Inputs may be any that keep to these rules, and one draw needn't show every extreme that they name: `batch_count`: some device has all 2048 rows live in every draw.
All inputs are finite; a program needn't handle non-finite values.
Results may differ from a plain program's by a relative error of at most 0.015.
Values may be sent and summed in bfloat16 or wider, within the bound.
A program may use at most 128 MiB of HBM per device.

v0:
```python
import jax
import jax.numpy as jnp
from jax import lax
from jax.sharding import PartitionSpec as P


def table_sums(index_cols, row_grad, table_rows, fanout):
    block = min(512, table_rows)
    blocks = table_rows // block
    offsets = jnp.arange(block, dtype=jnp.int32)

    def one_block(start):
        wanted = start + offsets
        counts = jnp.zeros((block, index_cols.shape[0]), jnp.float32)
        for column in range(index_cols.shape[1]):
            counts = counts + (index_cols[:, column][None, :] == wanted[:, None]).astype(
                jnp.float32
            )
        summed = jnp.dot(counts.astype(jnp.bfloat16), row_grad, preferred_element_type=jnp.float32)
        return (summed * (1.0 / fanout)).astype(jnp.bfloat16)

    starts = jnp.arange(blocks, dtype=jnp.int32) * block
    parts = lax.map(one_block, starts)
    return parts.reshape(table_rows, row_grad.shape[1])


def on_device(
    out_grad, pre_act, batch_count, layer_two, hot_slots, cold_index, hot_feats, cold_feats
):
    rows = out_grad.shape[0]
    hot_local = hot_feats.shape[0]
    hot_total = hot_local * lax.axis_size("clique")
    k_hot = hot_slots.shape[1]
    k_cold = cold_index.shape[1]
    fanout = k_hot + k_cold
    cold_rows = cold_feats.shape[0]
    live = (jnp.arange(rows, dtype=jnp.int32) < batch_count[0])[:, None]
    masked = jnp.where(live, out_grad, jnp.zeros_like(out_grad))
    activ = jnp.maximum(pre_act, jnp.zeros_like(pre_act))
    grad_two = jnp.dot(activ.T, masked, preferred_element_type=jnp.float32)
    back = jnp.dot(masked, layer_two.T, preferred_element_type=jnp.float32)
    row_grad = jnp.where(pre_act > 0, back, jnp.zeros_like(back)).astype(jnp.bfloat16)
    hot_part = table_sums(hot_slots, row_grad, hot_total, fanout)
    summed = lax.psum(hot_part, "clique").astype(jnp.float32)
    owned = lax.dynamic_slice_in_dim(summed, lax.axis_index("clique") * hot_local, hot_local, 0)
    cold_part = table_sums(cold_index, row_grad, cold_rows, fanout)
    grad_one = jnp.dot(cold_feats.T, cold_part, preferred_element_type=jnp.float32)
    grad_one = grad_one + jnp.dot(
        hot_feats.T, owned.astype(jnp.bfloat16), preferred_element_type=jnp.float32
    )
    total_one, total_two = lax.psum((grad_one, grad_two), ("clique", "copy"))
    return (total_one, total_two)


def solution(mesh):
    placed = (
        P(("clique", "copy"), None),
        P(("clique", "copy"), None),
        P(("clique", "copy")),
        P(),
        P(("clique", "copy"), None),
        P(("clique", "copy"), None),
        P("clique", None),
        P(("clique", "copy"), None),
    )
    return jax.shard_map(
        on_device, mesh=mesh, in_specs=placed, out_specs=(P(), P()), check_vma=False
    )
```

profile of v0, /device:TPU:2, one launch (start us, length us, event | category | flops | bytes accessed | tf_op | source)
XLA Modules:
  0.0 475.0 jit_solution(12058573302038147682)
XLA Ops:
  8.1 5.2 %select_convert_fusion = bf16[2048,512]{1,0:T(8,128)(2,1)} fusion(bf16[2048,512]{1,0:T(8,128)(2,1)} %param.13, bf16[512,512]{1,0:T(8,128)(2,1)} %param.15, bf16[2048,512]{1,0:T(8,128)(2,1)} %param.12, pred[2048]{0:T(1024)(128)(4,1)S(1)} %iota_compare_fusion), kind=kOutput, calls=%fused_computation.43 | convolution fusion | flops 1077936128 | bytes 6817792 | tf_op jit(solution)/shard_map/dot_general | solution.py:41
  13.2 63.4 %while.23 = (s32[]{:T(128)}, bf16[8,512,512]{2,1,0:T(8,128)(2,1)}, s32[2048,10]{0,1:T(8,128)S(1)}, s32[8]{0:T(128)S(1)}, bf16[2048,512]{1,0:T(8,128)(2,1)}, /*index=5*/s32[]{:T(128)}) while((s32[]{:T(128)}, bf16[8,512,512]{2,1,0:T(8,128)(2,1)}, s32[2048,10]{0,1:T(8,128)S(1)}, s32[8]{0:T(128)S(1)}, bf16[2048,512]{1,0:T(8,128)(2,1)}, ...), condition=%wide.region_3.4_spmd.clone, body=%wide.region_2.3_spmd.clone.sunk | while | flops 1105723904 | bytes 2871893 | solution.py:23
  13.3 0.6 dynamic_slice.22
  14.6 6.6 %fusion.68 = bf16[8,512,512]{2,1,0:T(8,128)(2,1)} fusion(bf16[8,512,512]{2,1,0:T(8,128)(2,1)} %get-tuple-element.278, s32[]{:T(128)} %get-tuple-element.277, bf16[2048,512]{1,0:T(8,128)(2,1)} %get-tuple-element.287, s32[2048]{0:T(1024)S(1)} %bitcast.126, s32[2048]{0:T(1024)S(1)} %bitcast.127, s32[2048]{0:T(1024)S(1)} %bitcast.128, ...), kind=kOutput, calls=%fused_computation.41.clone.1 | convolution fusion | flops 1105723392 | bytes 2705920 | tf_op jit(solution)/shard_map/while/body/eval_jaxpr/dot_general | solution.py:19
  21.2 0.6 dynamic_slice.22
  22.5 6.6 %fusion.68 = bf16[8,512,512]{2,1,0:T(8,128)(2,1)} fusion(bf16[8,512,512]{2,1,0:T(8,128)(2,1)} %get-tuple-element.278, s32[]{:T(128)} %get-tuple-element.277, bf16[2048,512]{1,0:T(8,128)(2,1)} %get-tuple-element.287, s32[2048]{0:T(1024)S(1)} %bitcast.126, s32[2048]{0:T(1024)S(1)} %bitcast.127, s32[2048]{0:T(1024)S(1)} %bitcast.128, ...), kind=kOutput, calls=%fused_computation.41.clone.1 | convolution fusion | flops 1105723392 | bytes 2705920 | tf_op jit(solution)/shard_map/while/body/eval_jaxpr/dot_general | solution.py:19
  29.2 0.6 dynamic_slice.22
  30.4 6.6 %fusion.68 = bf16[8,512,512]{2,1,0:T(8,128)(2,1)} fusion(bf16[8,512,512]{2,1,0:T(8,128)(2,1)} %get-tuple-element.278, s32[]{:T(128)} %get-tuple-element.277, bf16[2048,512]{1,0:T(8,128)(2,1)} %get-tuple-element.287, s32[2048]{0:T(1024)S(1)} %bitcast.126, s32[2048]{0:T(1024)S(1)} %bitcast.127, s32[2048]{0:T(1024)S(1)} %bitcast.128, ...), kind=kOutput, calls=%fused_computation.41.clone.1 | convolution fusion | flops 1105723392 | bytes 2705920 | tf_op jit(solution)/shard_map/while/body/eval_jaxpr/dot_general | solution.py:19
  37.1 0.6 dynamic_slice.22
  38.4 6.6 %fusion.68 = bf16[8,512,512]{2,1,0:T(8,128)(2,1)} fusion(bf16[8,512,512]{2,1,0:T(8,128)(2,1)} %get-tuple-element.278, s32[]{:T(128)} %get-tuple-element.277, bf16[2048,512]{1,0:T(8,128)(2,1)} %get-tuple-element.287, s32[2048]{0:T(1024)S(1)} %bitcast.126, s32[2048]{0:T(1024)S(1)} %bitcast.127, s32[2048]{0:T(1024)S(1)} %bitcast.128, ...), kind=kOutput, calls=%fused_computation.41.clone.1 | convolution fusion | flops 1105723392 | bytes 2705920 | tf_op jit(solution)/shard_map/while/body/eval_jaxpr/dot_general | solution.py:19
  45.0 0.6 dynamic_slice.22
  46.3 6.6 %fusion.68 = bf16[8,512,512]{2,1,0:T(8,128)(2,1)} fusion(bf16[8,512,512]{2,1,0:T(8,128)(2,1)} %get-tuple-element.278, s32[]{:T(128)} %get-tuple-element.277, bf16[2048,512]{1,0:T(8,128)(2,1)} %get-tuple-element.287, s32[2048]{0:T(1024)S(1)} %bitcast.126, s32[2048]{0:T(1024)S(1)} %bitcast.127, s32[2048]{0:T(1024)S(1)} %bitcast.128, ...), kind=kOutput, calls=%fused_computation.41.clone.1 | convolution fusion | flops 1105723392 | bytes 2705920 | tf_op jit(solution)/shard_map/while/body/eval_jaxpr/dot_general | solution.py:19
  52.9 0.6 dynamic_slice.22
  54.2 6.6 %fusion.68 = bf16[8,512,512]{2,1,0:T(8,128)(2,1)} fusion(bf16[8,512,512]{2,1,0:T(8,128)(2,1)} %get-tuple-element.278, s32[]{:T(128)} %get-tuple-element.277, bf16[2048,512]{1,0:T(8,128)(2,1)} %get-tuple-element.287, s32[2048]{0:T(1024)S(1)} %bitcast.126, s32[2048]{0:T(1024)S(1)} %bitcast.127, s32[2048]{0:T(1024)S(1)} %bitcast.128, ...), kind=kOutput, calls=%fused_computation.41.clone.1 | convolution fusion | flops 1105723392 | bytes 2705920 | tf_op jit(solution)/shard_map/while/body/eval_jaxpr/dot_general | solution.py:19
  60.9 0.6 dynamic_slice.22
  62.1 6.6 %fusion.68 = bf16[8,512,512]{2,1,0:T(8,128)(2,1)} fusion(bf16[8,512,512]{2,1,0:T(8,128)(2,1)} %get-tuple-element.278, s32[]{:T(128)} %get-tuple-element.277, bf16[2048,512]{1,0:T(8,128)(2,1)} %get-tuple-element.287, s32[2048]{0:T(1024)S(1)} %bitcast.126, s32[2048]{0:T(1024)S(1)} %bitcast.127, s32[2048]{0:T(1024)S(1)} %bitcast.128, ...), kind=kOutput, calls=%fused_computation.41.clone.1 | convolution fusion | flops 1105723392 | bytes 2705920 | tf_op jit(solution)/shard_map/while/body/eval_jaxpr/dot_general | solution.py:19
  68.8 0.6 dynamic_slice.22
  70.1 6.6 %fusion.68 = bf16[8,512,512]{2,1,0:T(8,128)(2,1)} fusion(bf16[8,512,512]{2,1,0:T(8,128)(2,1)} %get-tuple-element.278, s32[]{:T(128)} %get-tuple-element.277, bf16[2048,512]{1,0:T(8,128)(2,1)} %get-tuple-element.287, s32[2048]{0:T(1024)S(1)} %bitcast.126, s32[2048]{0:T(1024)S(1)} %bitcast.127, s32[2048]{0:T(1024)S(1)} %bitcast.128, ...), kind=kOutput, calls=%fused_computation.41.clone.1 | convolution fusion | flops 1105723392 | bytes 2705920 | tf_op jit(solution)/shard_map/while/body/eval_jaxpr/dot_general | solution.py:19
  77.0 4.6 fusion.41
  81.5 39.8 %while.22 = (s32[]{:T(128)}, bf16[4,512,512]{2,1,0:T(8,128)(2,1)}, s32[2048,15]{0,1:T(8,128)S(1)}, s32[4]{0:T(128)S(1)}, bf16[2048,512]{1,0:T(8,128)(2,1)}, /*index=5*/s32[]{:T(128)}) while((s32[]{:T(128)}, bf16[4,512,512]{2,1,0:T(8,128)(2,1)}, s32[2048,15]{0,1:T(8,128)S(1)}, s32[4]{0:T(128)S(1)}, bf16[2048,512]{1,0:T(8,128)(2,1)}, ...), condition=%wide.region_1.2_spmd.clone, body=%wide.region_0.1_spmd.clone.sunk | while | flops 1121452544 | bytes 2994773 | solution.py:23
  82.2 0.6 iota_add_fusion.4
  82.9 8.6 %fusion.65 = bf16[4,512,512]{2,1,0:T(8,128)(2,1)} fusion(bf16[4,512,512]{2,1,0:T(8,128)(2,1)} %get-tuple-element.260, s32[]{:T(128)} %get-tuple-element.259, bf16[2048,512]{1,0:T(8,128)(2,1)} %get-tuple-element.269, s32[2048]{0:T(1024)S(1)} %bitcast.111, s32[2048]{0:T(1024)S(1)} %bitcast.112, s32[2048]{0:T(1024)S(1)} %bitcast.113, ...), kind=kOutput, calls=%fused_computation.23.clone.1 | convolution fusion | flops 1121452032 | bytes 2746880 | tf_op jit(solution)/shard_map/while/body/eval_jaxpr/dot_general | solution.py:19
  92.2 0.6 iota_add_fusion.4
  92.9 8.6 %fusion.65 = bf16[4,512,512]{2,1,0:T(8,128)(2,1)} fusion(bf16[4,512,512]{2,1,0:T(8,128)(2,1)} %get-tuple-element.260, s32[]{:T(128)} %get-tuple-element.259, bf16[2048,512]{1,0:T(8,128)(2,1)} %get-tuple-element.269, s32[2048]{0:T(1024)S(1)} %bitcast.111, s32[2048]{0:T(1024)S(1)} %bitcast.112, s32[2048]{0:T(1024)S(1)} %bitcast.113, ...), kind=kOutput, calls=%fused_computation.23.clone.1 | convolution fusion | flops 1121452032 | bytes 2746880 | tf_op jit(solution)/shard_map/while/body/eval_jaxpr/dot_general | solution.py:19
  102.8 8.6 %fusion.65 = bf16[4,512,512]{2,1,0:T(8,128)(2,1)} fusion(bf16[4,512,512]{2,1,0:T(8,128)(2,1)} %get-tuple-element.260, s32[]{:T(128)} %get-tuple-element.259, bf16[2048,512]{1,0:T(8,128)(2,1)} %get-tuple-element.269, s32[2048]{0:T(1024)S(1)} %bitcast.111, s32[2048]{0:T(1024)S(1)} %bitcast.112, s32[2048]{0:T(1024)S(1)} %bitcast.113, ...), kind=kOutput, calls=%fused_computation.23.clone.1 | convolution fusion | flops 1121452032 | bytes 2746880 | tf_op jit(solution)/shard_map/while/body/eval_jaxpr/dot_general | solution.py:19
  112.8 8.6 %fusion.65 = bf16[4,512,512]{2,1,0:T(8,128)(2,1)} fusion(bf16[4,512,512]{2,1,0:T(8,128)(2,1)} %get-tuple-element.260, s32[]{:T(128)} %get-tuple-element.259, bf16[2048,512]{1,0:T(8,128)(2,1)} %get-tuple-element.269, s32[2048]{0:T(1024)S(1)} %bitcast.111, s32[2048]{0:T(1024)S(1)} %bitcast.112, s32[2048]{0:T(1024)S(1)} %bitcast.113, ...), kind=kOutput, calls=%fused_computation.23.clone.1 | convolution fusion | flops 1121452032 | bytes 2746880 | tf_op jit(solution)/shard_map/while/body/eval_jaxpr/dot_general | solution.py:19
  121.4 4.6 fusion.50
  126.0 66.5 %all-reduce.4.cloned.1.call-done = bf16[4096,512]{1,0:T(8,128)(2,1)} async-done(((bf16[4096,512]{1,0:T(8,128)(2,1)}), bf16[4096,512]{1,0:T(8,128)(2,1)}) %all-reduce.4.cloned.1.call-update) | async-done | bytes 4194320 | tf_op jit(solution)/shard_map/psum | solution.py:44
  192.5 3.6 add_bitcast_fusion
  196.0 266.8 %all-reduce.6.cloned.1.call-done = (f32[768,512]{0,1:T(8,128)}, f32[512,512]{1,0:T(8,128)}) async-done(((f32[768,512]{0,1:T(8,128)}, f32[512,512]{1,0:T(8,128)}), (f32[768,512]{0,1:T(8,128)}, f32[512,512]{1,0:T(8,128)})) %all-reduce.6.cloned.1.call-update) | async-done | bytes 2621456 | tf_op jit(solution)/shard_map/psum | solution.py:51
  462.9 3.0 copy.10
  465.9 2.3 copy.30
  (41 shorter events, 9.8 us)
Async XLA Ops:
  7.2 114.2 %copy-start = (bf16[2048,768]{1,0:T(8,128)(2,1)S(1)}, bf16[2048,768]{1,0:T(8,128)(2,1)}, u32[]{:S(2)}) copy-start(bf16[2048,768]{1,0:T(8,128)(2,1)} %param.19) | copy-start | bytes 9437188
  7.2 185.3 %all-reduce.4.cloned.1.call-start = ((), (), s32[]{:S(2)}) async-start(), calls=%async_computation | async-start | bytes 8388608 | tf_op jit(solution)/shard_map/psum | solution.py:44
  8.1 5.2 %copy-start.2 = (s32[2048,10]{0,1:T(8,128)S(1)}, s32[2048,10]{0,1:T(8,128)}, u32[]{:S(2)}) copy-start(s32[2048,10]{0,1:T(8,128)} %param.16) | copy-start | bytes 245764
  76.7 4.8 %copy-start.1 = (s32[2048,15]{0,1:T(8,128)S(1)}, s32[2048,15]{0,1:T(8,128)}, u32[]{:S(2)}) copy-start(s32[2048,15]{0,1:T(8,128)} %param.17) | copy-start | bytes 368644
  76.7 386.1 %all-reduce.6.cloned.1.call-start = ((), (), s32[]{:S(2)}) async-start(), calls=%async_computation.1 | async-start | bytes 5242880 | tf_op jit(solution)/shard_map/psum | solution.py:51
Sparse Core Ops, SparseCore 0:
  76.8 115.5 all-reduce.3
  198.6 264.2 all-reduce.5
where the time goes:
time: 476 us; the launch traced here: 475 us
  waiting for transfers between devices  333 us (70%)
  matrix products  105 us (22%)
  between operations  14.9 us (3%)
  local copies, waits for them, and re-layouts  13.6 us (3%)
  other arithmetic  7.56 us (2%)
    psum x1, waiting for transfers between devices, on_device(): total_one, total_two = lax.psum((grad_one, grad_two), ('clique', 'copy'))  267 us
    dot_general x12, matrix products, one_block(): jnp.dot(counts.astype(jnp.bfloat16), row_grad, preferred_element_type=jnp...  87.3 us
    psum x1, waiting for transfers between devices, on_device(): summed = lax.psum(hot_part, 'clique').astype(jnp.float32)  66.5 us
  transfers between devices with their start and end apart: 2, of which 2 were waited for; matrix products, arithmetic and copies ran while one was open for 10% of the time, Pallas kernels for 0%

commit v1 on v0

--- a/solution.py
+++ b/solution.py
@@ -41,7 +41,7 @@
     back = jnp.dot(masked, layer_two.T, preferred_element_type=jnp.float32)
     row_grad = jnp.where(pre_act > 0, back, jnp.zeros_like(back)).astype(jnp.bfloat16)
     hot_part = table_sums(hot_slots, row_grad, hot_total, fanout)
-    summed = lax.psum(hot_part, "clique").astype(jnp.float32)
+    summed = jnp.sum(lax.all_gather(hot_part, "clique"), axis=0).astype(jnp.float32)
     owned = lax.dynamic_slice_in_dim(summed, lax.axis_index("clique") * hot_local, hot_local, 0)
     cold_part = table_sums(cold_index, row_grad, cold_rows, fanout)
     grad_one = jnp.dot(cold_feats.T, cold_part, preferred_element_type=jnp.float32)

time: 476 us -> 717 us (1.51)
  waiting for transfers between devices: 333 us -> 560 us
  other arithmetic: 7.56 us -> 21.7 us
    all_gather x0 -> x1, waiting for transfers between devices: none -> 297 us  [on_device(): lax.all_gather(hot_part, 'clique')]
    psum x1 -> x0, waiting for transfers between devices: 66.5 us -> none  [on_device(): summed = lax.psum(hot_part, 'clique').astype(jnp.float32)]
    reduce_sum x0 -> x1, other arithmetic: none -> 14.2 us  [on_device(): jnp.sum(lax.all_gather(hot_part, 'clique'), axis=0).astype(jnp.float32)]
  transfers between devices with their start and end apart: 2 -> 2, of which waited for: 2 -> 2; matrix products, arithmetic and copies ran while one was open for 10% -> 7% of each run, Pallas kernels for 0% -> 0%
where the time goes in v1:
time: 717 us; the launch traced here: 716 us
  waiting for transfers between devices  560 us (78%)
  matrix products  106 us (15%)
  other arithmetic  21.7 us (3%)
  between operations  14.9 us (2%)
  local copies, waits for them, and re-layouts  13.6 us (2%)
    all_gather x1, waiting for transfers between devices, on_device(): lax.all_gather(hot_part, 'clique')  297 us
    psum x1, waiting for transfers between devices, on_device(): total_one, total_two = lax.psum((grad_one, grad_two), ('clique', 'copy'))  263 us
    dot_general x12, matrix products, one_block(): jnp.dot(counts.astype(jnp.bfloat16), row_grad, preferred_element_type=jnp...  87.9 us
  transfers between devices with their start and end apart: 2, of which 2 were waited for; matrix products, arithmetic and copies ran while one was open for 7% of the time, Pallas kernels for 0%

profile of v1, /device:TPU:2, one launch (start us, length us, event | category | flops | bytes accessed | tf_op | source)
XLA Modules:
  0.0 716.1 jit_solution(10865041712418734804)
XLA Ops:
  8.1 5.1 select_convert_fusion
  13.2 63.5 %while.23 = (s32[]{:T(128)}, bf16[8,512,512]{2,1,0:T(8,128)(2,1)}, s32[2048,10]{0,1:T(8,128)S(1)}, s32[8]{0:T(128)S(1)}, bf16[2048,512]{1,0:T(8,128)(2,1)}, /*index=5*/s32[]{:T(128)}) while((s32[]{:T(128)}, bf16[8,512,512]{2,1,0:T(8,128)(2,1)}, s32[2048,10]{0,1:T(8,128)S(1)}, s32[8]{0:T(128)S(1)}, bf16[2048,512]{1,0:T(8,128)(2,1)}, ...), condition=%wide.region_3.4_spmd.clone, body=%wide.region_2.3_spmd.clone.sunk | while | flops 1105723904 | bytes 2871393 | solution.py:23
  13.2 0.6 dynamic_slice.22
  13.9 0.6 iota_add_fusion.5
  14.5 6.6 fusion.68
  21.2 0.6 dynamic_slice.22
  22.4 6.6 fusion.68
  29.1 0.6 dynamic_slice.22
  30.4 6.6 fusion.68
  37.1 0.6 dynamic_slice.22
  38.4 6.6 fusion.68
  45.0 0.6 dynamic_slice.22
  46.3 6.6 fusion.68
  52.9 0.6 dynamic_slice.22
  54.2 6.6 fusion.68
  60.8 0.6 dynamic_slice.22
  62.1 6.6 fusion.68
  68.8 0.6 dynamic_slice.22
  70.0 6.6 fusion.68
  76.9 4.6 fusion.41
  81.5 40.4 %while.22 = (s32[]{:T(128)}, bf16[4,512,512]{2,1,0:T(8,128)(2,1)}, s32[2048,15]{0,1:T(8,128)S(1)}, s32[4]{0:T(128)S(1)}, bf16[2048,512]{1,0:T(8,128)(2,1)}, /*index=5*/s32[]{:T(128)}) while((s32[]{:T(128)}, bf16[4,512,512]{2,1,0:T(8,128)(2,1)}, s32[2048,15]{0,1:T(8,128)S(1)}, s32[4]{0:T(128)S(1)}, bf16[2048,512]{1,0:T(8,128)(2,1)}, ...), condition=%wide.region_1.2_spmd.clone, body=%wide.region_0.1_spmd.clone.sunk | while | flops 1121452544 | bytes 2994273 | solution.py:23
  82.8 8.7 %fusion.65 = bf16[4,512,512]{2,1,0:T(8,128)(2,1)} fusion(bf16[4,512,512]{2,1,0:T(8,128)(2,1)} %get-tuple-element.262, s32[]{:T(128)S(6)} %copy.16, bf16[2048,512]{1,0:T(8,128)(2,1)} %get-tuple-element.271, s32[2048]{0:T(1024)S(1)} %bitcast.111, s32[2048]{0:T(1024)S(1)} %bitcast.112, s32[2048]{0:T(1024)S(1)} %bitcast.113, s32[2048]{0:T(1024)S(1)} %bitcast.114, ...), kind=kOutput, calls=%fused_computation.23.clone.1 | convolution fusion | flops 1121452032 | bytes 2746372 | tf_op jit(solution)/shard_map/while/body/eval_jaxpr/dot_general | solution.py:19
  92.8 9.2 %fusion.65 = bf16[4,512,512]{2,1,0:T(8,128)(2,1)} fusion(bf16[4,512,512]{2,1,0:T(8,128)(2,1)} %get-tuple-element.262, s32[]{:T(128)S(6)} %copy.16, bf16[2048,512]{1,0:T(8,128)(2,1)} %get-tuple-element.271, s32[2048]{0:T(1024)S(1)} %bitcast.111, s32[2048]{0:T(1024)S(1)} %bitcast.112, s32[2048]{0:T(1024)S(1)} %bitcast.113, s32[2048]{0:T(1024)S(1)} %bitcast.114, ...), kind=kOutput, calls=%fused_computation.23.clone.1 | convolution fusion | flops 1121452032 | bytes 2746372 | tf_op jit(solution)/shard_map/while/body/eval_jaxpr/dot_general | solution.py:19
  103.3 8.6 %fusion.65 = bf16[4,512,512]{2,1,0:T(8,128)(2,1)} fusion(bf16[4,512,512]{2,1,0:T(8,128)(2,1)} %get-tuple-element.262, s32[]{:T(128)S(6)} %copy.16, bf16[2048,512]{1,0:T(8,128)(2,1)} %get-tuple-element.271, s32[2048]{0:T(1024)S(1)} %bitcast.111, s32[2048]{0:T(1024)S(1)} %bitcast.112, s32[2048]{0:T(1024)S(1)} %bitcast.113, s32[2048]{0:T(1024)S(1)} %bitcast.114, ...), kind=kOutput, calls=%fused_computation.23.clone.1 | convolution fusion | flops 1121452032 | bytes 2746372 | tf_op jit(solution)/shard_map/while/body/eval_jaxpr/dot_general | solution.py:19
  113.2 8.7 %fusion.65 = bf16[4,512,512]{2,1,0:T(8,128)(2,1)} fusion(bf16[4,512,512]{2,1,0:T(8,128)(2,1)} %get-tuple-element.262, s32[]{:T(128)S(6)} %copy.16, bf16[2048,512]{1,0:T(8,128)(2,1)} %get-tuple-element.271, s32[2048]{0:T(1024)S(1)} %bitcast.111, s32[2048]{0:T(1024)S(1)} %bitcast.112, s32[2048]{0:T(1024)S(1)} %bitcast.113, s32[2048]{0:T(1024)S(1)} %bitcast.114, ...), kind=kOutput, calls=%fused_computation.23.clone.1 | convolution fusion | flops 1121452032 | bytes 2746372 | tf_op jit(solution)/shard_map/while/body/eval_jaxpr/dot_general | solution.py:19
  121.9 4.6 fusion.50
  126.5 297.2 %all-gather.2.cloned.1.call-done = bf16[8,4096,512]{2,1,0:T(8,128)(2,1)} async-done(((bf16[1,4096,512]{2,1,0:T(8,128)(2,1)}), bf16[8,4096,512]{2,1,0:T(8,128)(2,1)}) %all-gather.2.cloned.1.call-update) | async-done | bytes 33554448 | tf_op jit(solution)/shard_map/all_gather | solution.py:44
  423.7 14.2 %reduce_sum.12 = bf16[4096,512]{1,0:T(8,128)(2,1)} reduce(bf16[8,4096,512]{2,1,0:T(8,128)(2,1)} %all-gather.2.cloned.1.call-done, bf16[]{:T(256)} %constant.14.clone.1), dimensions={0}, to_apply=%region_4.5 | reduce | flops 14680064 | bytes 37748736 | tf_op jit(solution)/shard_map/reduce_sum | solution.py:44
  437.9 3.6 add_bitcast_fusion
  441.5 262.5 %all-reduce.3.cloned.1.call-done = (f32[768,512]{0,1:T(8,128)}, f32[512,512]{1,0:T(8,128)}) async-done(((f32[768,512]{0,1:T(8,128)}, f32[512,512]{1,0:T(8,128)}), (f32[768,512]{0,1:T(8,128)}, f32[512,512]{1,0:T(8,128)})) %all-reduce.3.cloned.1.call-update) | async-done | bytes 2621456 | tf_op jit(solution)/shard_map/psum | solution.py:51
  704.0 3.0 copy.11
  707.0 2.3 copy.30
  (42 shorter events, 10.4 us)
Async XLA Ops:
  7.2 114.7 %copy-start = (bf16[2048,768]{1,0:T(8,128)(2,1)S(1)}, bf16[2048,768]{1,0:T(8,128)(2,1)}, u32[]{:S(2)}) copy-start(bf16[2048,768]{1,0:T(8,128)(2,1)} %param.19) | copy-start | bytes 9437188
  7.2 416.5 %all-gather.2.cloned.1.call-start = ((), (), s32[]{:S(2)}) async-start(), calls=%async_computation | async-start | bytes 37748736 | tf_op jit(solution)/shard_map/all_gather | solution.py:44
  8.1 5.1 copy-start.2
  76.7 4.8 copy-start.1
  76.7 627.4 %all-reduce.3.cloned.1.call-start = ((), (), s32[]{:S(2)}) async-start(), calls=%async_computation.1 | async-start | bytes 5242880 | tf_op jit(solution)/shard_map/psum | solution.py:51
Sparse Core Ops, SparseCore 0:
  76.8 346.8 all-gather.1
  441.6 262.3 all-reduce.2
